TPU v7x, 32 devices: a whole 2x2x4 slice. The times are simulated.
32 devices in a mesh: group: 2 (over x), ctx: 16 (over z, y, core).
Axes of the slice: x: 2, y: 2, z: 4, core: 2. Of those that a mesh axis runs over, the one named last changes fastest.
Arguments:
- normed_hidden: bfloat16 [4096, 8192], P(('group', 'ctx')), parts along dimension 0, may hold values from -6 to 6
- queries: bfloat16 [4096, 4096], P(('group', 'ctx')), parts along dimension 0, may hold values from -45 to 45
- keys: bfloat16 [4096, 512], P(('group', 'ctx')), parts along dimension 0, may hold values from -6 to 6
- value_frozen_matrix: bfloat16 [8192, 512], P('ctx'), may hold values from -0.0625 to 0.0625
- adapter_down_weight: bfloat16 [8192, 64], replicated, may hold values from -0.0625 to 0.0625
- adapter_up_weight: bfloat16 [64, 512], replicated, may hold values from -0.75 to 0.75
- block_slot_index: int32 [64], P(('group', 'ctx')), parts along dimension 0, may hold values from 0 to 31, each once
Outputs:
- attended: bfloat16 [4096, 4096], P(('group', 'ctx')), parts along dimension 0
There are 2 independent parts, one for each index of `group`. A program takes and returns all parts, laid end to end along the dimension named above; an argument that names none is the same for every part. Nothing has to cross between parts.
Inputs may be any that keep to these rules, and one draw needn't show every extreme that they name: `block_slot_index`: each of the 32 blocks is named once; slot j holds rows j*64 to (j+1)*64 - 1.
All inputs are finite; a program needn't handle non-finite values.
Results may differ from a plain program's by a relative error of at most 0.0054.
Values may be sent and summed in bfloat16 or wider, within the bound.
No kernel may reach another device: no remote copies, remote signals or barrier semaphores. Data moves between devices by JAX's collectives and lax.ppermute only.
A program may use at most 192 MiB of HBM per device.

v0:
```python
import jax
import jax.numpy as jnp
from jax import lax
from jax.sharding import PartitionSpec as P

QH = 32
KVH = 4
HD = 128
BLK = 64


def shards(
    normed_hidden,
    queries,
    keys,
    value_frozen_matrix,
    adapter_down_weight,
    adapter_up_weight,
    block_slot_index,
):
    tokens = normed_hidden.shape[0]
    scale = 1.0 / HD**0.5
    offsets = jnp.arange(BLK, dtype=jnp.int32)
    table = lax.all_gather(block_slot_index, "ctx", axis=0, tiled=True)
    my_pos = (block_slot_index[:, None] * BLK + offsets[None, :]).reshape(tokens)
    frozen_output = jnp.dot(
        normed_hidden,
        lax.all_gather(value_frozen_matrix, "ctx", axis=0, tiled=True),
        preferred_element_type=jnp.float32,
    )
    low_rank_output = jnp.dot(
        normed_hidden, adapter_down_weight, preferred_element_type=jnp.float32
    ).astype(jnp.bfloat16)
    value_output = (
        frozen_output
        + 0.5 * jnp.dot(low_rank_output, adapter_up_weight, preferred_element_type=jnp.float32)
    ).astype(jnp.bfloat16)
    slots_here = tokens // BLK
    query_slots = [
        queries[which * BLK : (which + 1) * BLK].reshape(BLK, KVH, QH // KVH, HD)
        for which in range(slots_here)
    ]
    pos_slots = [my_pos[which * BLK : (which + 1) * BLK] for which in range(slots_here)]
    shape_stat = (KVH, QH // KVH, BLK)
    init = tuple(
        (
            (
                jnp.full(shape_stat, -1e30, jnp.float32),
                jnp.zeros(shape_stat, jnp.float32),
                jnp.zeros(shape_stat + (HD,), jnp.float32),
            )
            for which in range(slots_here)
        )
    )
    key_piece = lax.all_gather(keys, "ctx", axis=0, tiled=True)
    count = key_piece.shape[0]
    key_pos = (table[:, None] * BLK + offsets[None, :]).reshape(count)
    key_three = key_piece.reshape(count, KVH, HD)
    value_three = lax.all_gather(value_output, "ctx", axis=0, tiled=True).reshape(count, KVH, HD)
    lowest_key = jnp.min(key_pos)
    updated = []
    for attend_which in range(slots_here):
        q_part = query_slots[attend_which]
        q_pos = pos_slots[attend_which]

        def update(state, q_part=q_part, q_pos=q_pos):
            top, total, accum = state
            scores = (
                jnp.einsum("tkgd,skd->kgts", q_part, key_three, preferred_element_type=jnp.float32)
                * scale
            )
            visible = (q_pos[:, None] >= key_pos[None, :])[None, None]
            scores = jnp.where(visible, scores, -1e30)
            top_new = jnp.maximum(top, jnp.max(scores, axis=-1))
            weights = jnp.where(visible, jnp.exp(scores - top_new[..., None]), 0.0)
            total = jnp.sum(weights, axis=-1)
            accum = jnp.einsum(
                "kgts,skd->kgtd",
                weights.astype(jnp.bfloat16),
                value_three,
                preferred_element_type=jnp.float32,
            )
            return (top_new, total, accum)

        def keep(state):
            return state

        updated.append(lax.cond(lowest_key <= jnp.max(q_pos), update, keep, init[attend_which]))
    states = tuple(updated)
    outputs = []
    for which in range(slots_here):
        result = states[which][2] / states[which][1][..., None]
        outputs.append(
            jnp.transpose(result, (2, 0, 1, 3)).reshape(BLK, QH * HD).astype(jnp.bfloat16)
        )
    return jnp.concatenate(outputs, axis=0)


def solution(mesh):
    in_specs = (
        P(("group", "ctx"), None),
        P(("group", "ctx"), None),
        P(("group", "ctx"), None),
        P("ctx", None),
        P(),
        P(),
        P(("group", "ctx")),
    )
    out_specs = P(("group", "ctx"), None)
    return jax.shard_map(shards, mesh=mesh, in_specs=in_specs, out_specs=out_specs, check_vma=False)
```

profile of v0, /device:TPU:0, one launch (start us, length us, event | category | flops | bytes accessed | tf_op | source)
XLA Modules:
  0.0 216.8 jit_solution(570349210918793714)
XLA Ops:
  6.5 0.0 copy-start
  6.5 0.0 copy-start.6
  6.5 0.0 copy-start.3
  6.5 0.0 copy-start.4
  6.5 0.0 copy-start.5
  6.5 0.0 all-gather.6.cloned.1.call-start
  6.6 0.7 all-gather.6.cloned.1.call-update
  7.3 0.0 all-gather.8.cloned.1.call-start
  7.3 79.2 %all-gather.6.cloned.1.call-done = bf16[8192,512]{1,0:T(8,128)(2,1)} async-done(((bf16[512,512]{1,0:T(8,128)(2,1)}), bf16[8192,512]{1,0:T(8,128)(2,1)}) %all-gather.6.cloned.1.call-update) | async-done | bytes 8388624 | tf_op jit(solution)/shard_map/all_gather | solution.py:28
  86.6 0.0 copy-done
  86.6 4.6 %fusion.31 = f32[128,512]{1,0:T(8,128)S(1)} fusion(bf16[128,8192]{1,0:T(8,128)(2,1)S(1)} %copy-done, bf16[8192,512]{1,0:T(8,128)(2,1)} %all-gather.6.cloned.1.call-done), kind=kOutput, calls=%fused_computation.52 | convolution fusion | flops 1073741824 | bytes 10747904 | tf_op jit(solution)/shard_map/dot_general | solution.py:26
  91.2 0.0 copy-done.3
  91.2 2.4 %fusion.27 = bf16[128,512]{1,0:T(8,128)(2,1)} fusion(f32[128,512]{1,0:T(8,128)S(1)} %fusion.31, bf16[64,512]{1,0:T(8,128)(2,1)} %param.16, bf16[128,8192]{1,0:T(8,128)(2,1)S(1)} %copy-done, bf16[8192,64]{0,1:T(8,128)(2,1)S(1)} %copy-done.3), kind=kOutput, calls=%fused_computation.36 | convolution fusion | flops 142811136 | bytes 3604480 | tf_op jit(solution)/shard_map/dot_general | solution.py:36
  93.6 0.0 all-gather.8.cloned.1.call-update
  93.6 0.0 all-gather.4.cloned.1.call-start
  93.7 0.0 copy-done.4
  93.7 0.8 copy.14
  94.4 0.0 all-gather.4.cloned.1.call-update
  94.5 0.0 copy-done.6
  94.5 0.6 dynamic-slice
  95.6 0.0 copy-done.5
  95.6 0.2 dynamic-update-slice
  95.9 9.9 %all-reduce = s32[32]{0:T(128)S(1)} all-reduce(s32[32]{0:T(128)S(1)} %dynamic-update-slice), channel_id=1, replica_groups=mesh['group'=2,'ctx'=16] {'ctx'}, use_global_device_ids=true, to_apply=%add | all-reduce | flops 32 | bytes 256
  105.8 0.1 iota_add_fusion.1
  105.9 0.7 slice_reduce_fusion.1
  106.6 0.7 iota_add_fusion
  109.7 24.1 %all-gather.8.cloned.1.call-done = bf16[2048,512]{1,0:T(8,128)(2,1)} async-done(((bf16[128,512]{1,0:T(8,128)(2,1)}), bf16[2048,512]{1,0:T(8,128)(2,1)}) %all-gather.8.cloned.1.call-update) | async-done | bytes 2097168 | tf_op jit(solution)/shard_map/all_gather | solution.py:59
  133.7 4.0 %reshape.101 = bf16[2048,4,128]{2,1,0:T(4,128)(2,1)} reshape(bf16[2048,512]{1,0:T(8,128)(2,1)} %all-gather.8.cloned.1.call-done) | data formatting | bytes 4194304 | tf_op jit(solution)/shard_map/reshape | solution.py:59
  137.7 38.0 %all-gather.4.cloned.1.call-done = bf16[2048,512]{0,1:T(8,128)(2,1)} async-done(((bf16[128,512]{0,1:T(8,128)(2,1)}), bf16[2048,512]{0,1:T(8,128)(2,1)}) %all-gather.4.cloned.1.call-update) | async-done | bytes 2097168 | tf_op jit(solution)/shard_map/all_gather | solution.py:55
  175.7 14.9 %conditional.2 = (f32[4,8,64]{2,1,0:T(8,128)S(1)}, f32[4,8,64,128]{3,2,1,0:T(8,128)S(1)}) conditional(s32[]{:T(128)} %convert_element_type.36, () %tuple.21, (s32[1,64]{1,0:T(1,128)S(1)}, s32[32,64]{1,0:T(8,128)S(1)}, bf16[128,4096]{1,0:T(8,128)(2,1)}, bf16[2048,4,128]{0,2,1:T(8,128)(2,1)}, bf16[2048,4,128]{2,1,0:T(4,128)(2,1)}) %tuple.46), branch_computations={%region_2.0_spmd, %region_3.6_spmd} | conditional | flops 2202138624 | bytes 67182896 | solution.py:88
  175.7 0.1 ge.34
  175.8 0.0 copy-start.1
  175.8 0.1 broadcast_compare_fusion
  175.9 1.2 slice_bitcast_fusion
  177.1 0.1 copy.33
  177.2 4.4 %fusion = (f32[4,8,64]{2,1,0:T(8,128)S(1)}, f32[4,2048,64,8]{1,2,3,0:T(8,128)S(1)}) fusion(pred[64,2048]{1,0:T(8,128)(4,1)S(1)} %broadcast_compare_fusion, bf16[64,4,8,128]{3,2,1,0:T(8,128)(2,1)S(1)} %bitcast.69, bf16[2048,4,128]{0,2,1:T(8,128)(2,1)} %get-tuple-element.62), kind=kOutput, calls=%fused_computation.2 | convolution fusion | flops 1086322688 | bytes 19537920 | tf_op jit(solution)/shard_map/cond/branch_1_fun/tkgd,skd->kgts/dot_general | solution.py:69
  181.7 0.0 copy-done.1
  181.7 3.8 %fusion.3 = f32[4,8,64,128]{3,2,1,0:T(8,128)S(1)} fusion(f32[4,2048,64,8]{1,2,3,0:T(8,128)S(1)} %get-tuple-element.72, f32[4,8,64]{2,1,0:T(8,128)S(1)} %broadcast_maximum_fusion, pred[64,2048]{1,0:T(8,128)(4,1)S(1)} %broadcast_compare_fusion, bf16[2048,4,128,1]{2,1,0,3:T(4,128)(2,1)S(1)} %bitcast.71), kind=kOutput, calls=%fused_computation.5 | convolution fusion | flops 1094713344 | bytes 20062208 | tf_op jit(solution)/shard_map/cond/branch_1_fun/kgts,skd->kgtd/dot_general | solution.py:77
  185.5 5.1 %fusion.2 = f32[4,8,64]{2,1,0:T(8,128)S(1)} fusion(f32[4,2048,64,8]{1,2,3,0:T(8,128)S(1)} %get-tuple-element.72, f32[4,8,64]{2,1,0:T(8,128)S(1)} %broadcast_maximum_fusion, pred[64,2048]{1,0:T(8,128)(4,1)S(1)} %broadcast_compare_fusion), kind=kLoop, calls=%fused_computation.4 | loop fusion | flops 20969472 | bytes 16924672 | tf_op jit(solution)/shard_map/cond/branch_1_fun/reduce_sum | solution.py:76
  190.6 0.3 fusion.28
  191.0 1.1 copy.17
  192.1 14.9 %conditional.3 = (f32[4,8,64]{2,1,0:T(8,128)S(1)}, f32[4,8,64,128]{3,2,1,0:T(8,128)S(1)}) conditional(s32[]{:T(128)} %convert_element_type.42, () %tuple.23, (s32[1,64]{1,0:T(1,128)S(1)}, s32[32,64]{1,0:T(8,128)S(1)}, bf16[128,4096]{1,0:T(8,128)(2,1)}, bf16[2048,4,128]{0,2,1:T(8,128)(2,1)}, bf16[2048,4,128]{2,1,0:T(4,128)(2,1)}) %tuple.47), branch_computations={%region_7.8_spmd, %region_8.11_spmd} | conditional | flops 2202138624 | bytes 67182896 | solution.py:88
  192.1 0.1 ge.39
  192.2 0.0 copy-start.2
  192.2 0.1 broadcast_compare_fusion.1
  192.3 1.2 slice_bitcast_fusion.1
  193.6 0.1 copy.34
  193.6 4.4 %fusion.13 = (f32[4,8,64]{2,1,0:T(8,128)S(1)}, f32[4,2048,64,8]{1,2,3,0:T(8,128)S(1)}) fusion(pred[64,2048]{1,0:T(8,128)(4,1)S(1)} %broadcast_compare_fusion.1, bf16[64,4,8,128]{3,2,1,0:T(8,128)(2,1)S(1)} %bitcast.70, bf16[2048,4,128]{0,2,1:T(8,128)(2,1)} %get-tuple-element.67), kind=kOutput, calls=%fused_computation.19 | convolution fusion | flops 1086322688 | bytes 19537920 | tf_op jit(solution)/shard_map/cond/branch_1_fun/tkgd,skd->kgts/dot_general | solution.py:69
  198.1 0.0 copy-done.2
  198.1 3.8 %fusion.16 = f32[4,8,64,128]{3,2,1,0:T(8,128)S(1)} fusion(f32[4,2048,64,8]{1,2,3,0:T(8,128)S(1)} %get-tuple-element.74, f32[4,8,64]{2,1,0:T(8,128)S(1)} %broadcast_maximum_fusion.1, pred[64,2048]{1,0:T(8,128)(4,1)S(1)} %broadcast_compare_fusion.1, bf16[2048,4,128,1]{2,1,0,3:T(4,128)(2,1)S(1)} %bitcast.72), kind=kOutput, calls=%fused_computation.22 | convolution fusion | flops 1094713344 | bytes 20062208 | tf_op jit(solution)/shard_map/cond/branch_1_fun/kgts,skd->kgtd/dot_general | solution.py:77
  202.0 5.1 %fusion.15 = f32[4,8,64]{2,1,0:T(8,128)S(1)} fusion(f32[4,2048,64,8]{1,2,3,0:T(8,128)S(1)} %get-tuple-element.74, f32[4,8,64]{2,1,0:T(8,128)S(1)} %broadcast_maximum_fusion.1, pred[64,2048]{1,0:T(8,128)(4,1)S(1)} %broadcast_compare_fusion.1), kind=kLoop, calls=%fused_computation.21 | loop fusion | flops 20969472 | bytes 16924672 | tf_op jit(solution)/shard_map/cond/branch_1_fun/reduce_sum | solution.py:76
  207.1 0.3 fusion.29
  207.4 0.3 copy.20
  207.8 1.4 copy_bitcast_fusion
  209.2 1.1 pad_maximum_fusion
  (5 shorter events, 0.0 us)
Async XLA Ops:
  6.5 80.0 %copy-start = (bf16[128,8192]{1,0:T(8,128)(2,1)S(1)}, bf16[128,8192]{1,0:T(8,128)(2,1)}, u32[]{:S(2)}) copy-start(bf16[128,8192]{1,0:T(8,128)(2,1)} %param.11) | copy-start | bytes 6291460
  6.5 87.9 %copy-start.6 = (u32[32]{0:T(128)S(1)}, u32[32]{0:T(128)}, u32[]{:S(2)}) copy-start(u32[32]{0:T(128)} %constant.9) | copy-start | bytes 388
  6.5 84.7 %copy-start.3 = (bf16[8192,64]{0,1:T(8,128)(2,1)S(1)}, bf16[8192,64]{0,1:T(8,128)(2,1)}, u32[]{:S(2)}) copy-start(bf16[8192,64]{0,1:T(8,128)(2,1)} %param.15) | copy-start | bytes 3145732
  6.5 87.1 %copy-start.4 = (bf16[128,512]{1,0:T(8,128)(2,1)S(1)}, bf16[128,512]{1,0:T(8,128)(2,1)}, u32[]{:S(2)}) copy-start(bf16[128,512]{1,0:T(8,128)(2,1)} %param.13) | copy-start | bytes 393220
  6.5 89.1 %copy-start.5 = (s32[2]{0:T(128)S(1)}, s32[2]{0:T(128)}, u32[]{:S(2)}) copy-start(s32[2]{0:T(128)} %param.17) | copy-start | bytes 28
  6.5 80.0 %all-gather.6.cloned.1.call-start = ((), (), s32[]{:S(2)}) async-start(), calls=%async_computation.1 | async-start | bytes 8912896 | tf_op jit(solution)/shard_map/all_gather | solution.py:28
  7.3 126.5 %all-gather.8.cloned.1.call-start = ((), (), s32[]{:S(2)}) async-start(), calls=%async_computation.2 | async-start | bytes 2228224 | tf_op jit(solution)/shard_map/all_gather | solution.py:59
  93.6 82.1 %all-gather.4.cloned.1.call-start = ((), (), s32[]{:S(2)}) async-start(), calls=%async_computation | async-start | bytes 2228224 | tf_op jit(solution)/shard_map/all_gather | solution.py:55
  175.8 5.9 %copy-start.1 = (bf16[2048,4,128]{2,1,0:T(4,128)(2,1)S(1)}, bf16[2048,4,128]{2,1,0:T(4,128)(2,1)}, u32[]{:S(2)}) copy-start(bf16[2048,4,128]{2,1,0:T(4,128)(2,1)} %get-tuple-element.63) | copy-start | bytes 6291460 | tf_op jit(solution)/shard_map/cond
  192.2 5.9 %copy-start.2 = (bf16[2048,4,128]{2,1,0:T(4,128)(2,1)S(1)}, bf16[2048,4,128]{2,1,0:T(4,128)(2,1)}, u32[]{:S(2)}) copy-start(bf16[2048,4,128]{2,1,0:T(4,128)(2,1)} %get-tuple-element.68) | copy-start | bytes 6291460 | tf_op jit(solution)/shard_map/cond
Sparse Core Ops, SparseCore 0:
  9.5 77.0 all-gather.5
  93.7 39.9 all-gather.7
  135.9 39.7 all-gather.3
where the time goes:
time: 217 us
  waiting for transfers between devices  142 us (65%)
  matrix products  23.5 us (11%)
  between operations  16.1 us (7%)
  other arithmetic  13.7 us (6%)
  local copies, waits for them, and re-layouts  11.2 us (5%)
  blocking collectives  9.93 us (5%)
    all_gather x1, waiting for transfers between devices, shards(): lax.all_gather(value_frozen_matrix, 'ctx', axis=0, tiled=True)  79.2 us
    all_gather x1, waiting for transfers between devices, shards(): key_piece = lax.all_gather(keys, 'ctx', axis=0, tiled=True)  38 us
    all_gather x1, waiting for transfers between devices, shards(): lax.all_gather(value_output, 'ctx', axis=0, tiled=True)  24.1 us
    reduce_sum x2, other arithmetic, update(): total = jnp.sum(weights, axis=-1)  10.2 us
    unnamed x1, blocking collectives  9.93 us
    dot_general x2, matrix products, update(): jnp.einsum('tkgd,skd->kgts', q_part, key_three, preferred_element_type=jn...  8.88 us
    dot_general x2, matrix products, update(): jnp.einsum('kgts,skd->kgtd', weights.astype(jnp.bfloat16), value_three, p...  7.67 us
    dot_general x1, matrix products, shards(): jnp.dot(normed_hidden, lax.all_gather(value_frozen_matrix, 'ctx', axis=0,...  4.63 us
  transfers between devices with their start and end apart: 3, of which 3 were waited for; matrix products, arithmetic and copies ran while one was open for 3% of the time, Pallas kernels for 0%

commit v1 on v0

--- a/solution.py
+++ b/solution.py
@@ -23,9 +23,27 @@
     offsets = jnp.arange(BLK, dtype=jnp.int32)
     table = lax.all_gather(block_slot_index, "ctx", axis=0, tiled=True)
     my_pos = (block_slot_index[:, None] * BLK + offsets[None, :]).reshape(tokens)
+
+    def post_teams(shard_in, axis_key, ndim_at):
+        later = lax.psum(1, axis_key)
+        z2, piece_out, arr_out = (later, lax.axis_index(axis_key), shard_in.shape[ndim_at])
+        w2 = jnp.zeros(
+            [idx * z2 if hop_no == ndim_at else idx for hop_no, idx in enumerate(shard_in.shape)],
+            shard_in.dtype,
+        )
+        work_now = lax.dynamic_update_slice_in_dim(w2, shard_in, piece_out * arr_out, axis=ndim_at)
+        for k in range(1, z2):
+            shard_in = lax.ppermute(
+                shard_in, axis_key, list(map(lambda hop_no: (hop_no, (hop_no + 1) % z2), range(z2)))
+            )
+            work_now = lax.dynamic_update_slice_in_dim(
+                work_now, shard_in, (piece_out - k) % z2 * arr_out, axis=ndim_at
+            )
+        return work_now
+
     frozen_output = jnp.dot(
         normed_hidden,
-        lax.all_gather(value_frozen_matrix, "ctx", axis=0, tiled=True),
+        post_teams(value_frozen_matrix, axis_key="ctx", ndim_at=0),
         preferred_element_type=jnp.float32,
     )
     low_rank_output = jnp.dot(

time: 217 us -> 279 us (1.29)
  waiting for transfers between devices: 142 us -> 174 us
  local copies, waits for them, and re-layouts: 11.2 us -> 38.6 us
    ppermute x0 -> x15, waiting for transfers between devices: none -> 150 us  [post_teams(): lax.ppermute(shard_in, axis_key, list(map(lambda hop_no: (hop_no, (hop_no...]
    all_gather x1 -> x0, waiting for transfers between devices: 79.2 us -> none  [shards(): lax.all_gather(value_frozen_matrix, 'ctx', axis=0, tiled=True)]
    all_gather x1, waiting for transfers between devices: 38 us -> 0.02 us  [shards(): key_piece = lax.all_gather(keys, 'ctx', axis=0, tiled=True)]
    dynamic_update_slice x0 -> x16, local copies, waits for them, and re-layouts: none -> 24.9 us  [the longest x15 24 us: post_teams(): lax.dynamic_update_slice_in_dim(work_now, shard_in, (piece_out - k) % z2...]
    unnamed x14 -> x28, local copies, waits for them, and re-layouts: 1.6 us -> 6.61 us
    reshape x1 -> x0, local copies, waits for them, and re-layouts: 3.96 us -> none  [shards(): lax.all_gather(value_output, 'ctx', axis=0, tiled=True)]
    broadcast_in_dim x0 -> x1, local copies, waits for them, and re-layouts: none -> 3.77 us  [post_teams(): jnp.zeros([idx * z2 if hop_no == ndim_at else idx for hop_no, idx in enum...]
  transfers between devices with their start and end apart: 3 -> 17, of which waited for: 3 -> 16; matrix products, arithmetic and copies ran while one was open for 3% -> 15% of each run, Pallas kernels for 0% -> 0%
where the time goes in v1:
time: 279 us; the launch traced here: 278 us
  waiting for transfers between devices  174 us (62%)
  local copies, waits for them, and re-layouts  38.6 us (14%)
  matrix products  24.9 us (9%)
  between operations  16.7 us (6%)
  other arithmetic  13.7 us (5%)
  blocking collectives  9.14 us (3%)
    ppermute x15, waiting for transfers between devices, post_teams(): lax.ppermute(shard_in, axis_key, list(map(lambda hop_no: (hop_no, (hop_no...  150 us
    all_gather x1, waiting for transfers between devices, shards(): lax.all_gather(value_output, 'ctx', axis=0, tiled=True)  24.6 us
    dynamic_update_slice x15, local copies, waits for them, and re-layouts, post_teams(): lax.dynamic_update_slice_in_dim(work_now, shard_in, (piece_out - k) % z2...  24 us
    reduce_sum x2, other arithmetic, update(): total = jnp.sum(weights, axis=-1)  10.1 us
    dot_general x2, matrix products, update(): jnp.einsum('tkgd,skd->kgts', q_part, key_three, preferred_element_type=jn...  9.16 us
    unnamed x1, blocking collectives  9.14 us
    dot_general x2, matrix products, update(): jnp.einsum('kgts,skd->kgtd', weights.astype(jnp.bfloat16), value_three, p...  7.09 us
    unnamed x28, local copies, waits for them, and re-layouts  6.61 us
  transfers between devices with their start and end apart: 17, of which 16 were waited for; matrix products, arithmetic and copies ran while one was open for 15% of the time, Pallas kernels for 0%

profile of v1, /device:TPU:0, one launch (start us, length us, event | category | flops | bytes accessed | tf_op | source)
XLA Modules:
  0.0 278.0 jit_solution(9530320700059188844)
XLA Ops:
  6.5 0.5 collective-permute-start
  7.0 12.1 %collective-permute-done = bf16[512,512]{1,0:T(8,128)(2,1)S(1)} collective-permute-done((bf16[512,512]{1,0:T(8,128)(2,1)}, bf16[512,512]{1,0:T(8,128)(2,1)S(1)}, u32[]{:S(2)}, u32[]{:S(2)}) %collective-permute-start) | collective-permute-done | bytes 524320 | tf_op jit(solution)/shard_map/ppermute | solution.py:36
  19.1 11.4 %collective-permute-done.1 = bf16[512,512]{1,0:T(8,128)(2,1)} collective-permute-done((bf16[512,512]{1,0:T(8,128)(2,1)S(1)}, bf16[512,512]{1,0:T(8,128)(2,1)}, u32[]{:S(2)}, u32[]{:S(2)}) %collective-permute-start.1) | collective-permute-done | bytes 524320 | tf_op jit(solution)/shard_map/ppermute | solution.py:36
  30.5 11.6 %collective-permute-done.2 = bf16[512,512]{1,0:T(8,128)(2,1)} collective-permute-done((bf16[512,512]{1,0:T(8,128)(2,1)}, bf16[512,512]{1,0:T(8,128)(2,1)}, u32[]{:S(2)}, u32[]{:S(2)}) %collective-permute-start.2) | collective-permute-done | bytes 524320 | tf_op jit(solution)/shard_map/ppermute | solution.py:36
  42.2 11.5 %collective-permute-done.3 = bf16[512,512]{1,0:T(8,128)(2,1)S(1)} collective-permute-done((bf16[512,512]{1,0:T(8,128)(2,1)}, bf16[512,512]{1,0:T(8,128)(2,1)S(1)}, u32[]{:S(2)}, u32[]{:S(2)}) %collective-permute-start.3) | collective-permute-done | bytes 524320 | tf_op jit(solution)/shard_map/ppermute | solution.py:36
  53.7 0.8 copy-done.5
  54.5 10.6 %collective-permute-done.4 = bf16[512,512]{1,0:T(8,128)(2,1)} collective-permute-done((bf16[512,512]{1,0:T(8,128)(2,1)S(1)}, bf16[512,512]{1,0:T(8,128)(2,1)}, u32[]{:S(2)}, u32[]{:S(2)}) %collective-permute-start.4) | collective-permute-done | bytes 524320 | tf_op jit(solution)/shard_map/ppermute | solution.py:36
  65.1 11.5 %collective-permute-done.5 = bf16[512,512]{1,0:T(8,128)(2,1)S(1)} collective-permute-done((bf16[512,512]{1,0:T(8,128)(2,1)}, bf16[512,512]{1,0:T(8,128)(2,1)S(1)}, u32[]{:S(2)}, u32[]{:S(2)}) %collective-permute-start.5) | collective-permute-done | bytes 524320 | tf_op jit(solution)/shard_map/ppermute | solution.py:36
  76.6 0.8 copy-done.4
  77.4 11.3 %collective-permute-done.6 = bf16[512,512]{1,0:T(8,128)(2,1)S(1)} collective-permute-done((bf16[512,512]{1,0:T(8,128)(2,1)S(1)}, bf16[512,512]{1,0:T(8,128)(2,1)S(1)}, u32[]{:S(2)}, u32[]{:S(2)}) %collective-permute-start.6) | collective-permute-done | bytes 524320 | tf_op jit(solution)/shard_map/ppermute | solution.py:36
  88.7 0.8 copy-done.6
  89.5 11.3 %collective-permute-done.7 = bf16[512,512]{1,0:T(8,128)(2,1)S(1)} collective-permute-done((bf16[512,512]{1,0:T(8,128)(2,1)S(1)}, bf16[512,512]{1,0:T(8,128)(2,1)S(1)}, u32[]{:S(2)}, u32[]{:S(2)}) %collective-permute-start.7) | collective-permute-done | bytes 524320 | tf_op jit(solution)/shard_map/ppermute | solution.py:36
  100.8 0.8 copy-done.7
  101.6 11.3 %collective-permute-done.8 = bf16[512,512]{1,0:T(8,128)(2,1)S(1)} collective-permute-done((bf16[512,512]{1,0:T(8,128)(2,1)S(1)}, bf16[512,512]{1,0:T(8,128)(2,1)S(1)}, u32[]{:S(2)}, u32[]{:S(2)}) %collective-permute-start.8) | collective-permute-done | bytes 524320 | tf_op jit(solution)/shard_map/ppermute | solution.py:36
  112.9 0.8 copy-done.8
  113.8 11.4 %collective-permute-done.9 = bf16[512,512]{1,0:T(8,128)(2,1)} collective-permute-done((bf16[512,512]{1,0:T(8,128)(2,1)S(1)}, bf16[512,512]{1,0:T(8,128)(2,1)}, u32[]{:S(2)}, u32[]{:S(2)}) %collective-permute-start.9) | collective-permute-done | bytes 524320 | tf_op jit(solution)/shard_map/ppermute | solution.py:36
  125.2 1.7 copy.15
  126.9 9.9 %collective-permute-done.10 = bf16[512,512]{1,0:T(8,128)(2,1)} collective-permute-done((bf16[512,512]{1,0:T(8,128)(2,1)}, bf16[512,512]{1,0:T(8,128)(2,1)}, u32[]{:S(2)}, u32[]{:S(2)}) %collective-permute-start.10) | collective-permute-done | bytes 524320 | tf_op jit(solution)/shard_map/ppermute | solution.py:36
  136.8 2.1 convolution_multiply_fusion
  139.0 13.0 %collective-permute-done.11 = bf16[512,512]{1,0:T(8,128)(2,1)} collective-permute-done((bf16[512,512]{1,0:T(8,128)(2,1)}, bf16[512,512]{1,0:T(8,128)(2,1)}, u32[]{:S(2)}, u32[]{:S(2)}) %collective-permute-start.11) | collective-permute-done | bytes 524320 | tf_op jit(solution)/shard_map/ppermute | solution.py:36
  152.0 3.8 %broadcast_in_dim.47 = bf16[8192,512]{1,0:T(8,128)(2,1)} broadcast(bf16[]{:T(256)} %constant.135.clone.1), dimensions={} | broadcast | bytes 8388610 | tf_op jit(solution)/shard_map/broadcast_in_dim | solution.py:30
  155.8 0.8 constant_dynamic-update-slice_fusion.15
  156.6 0.9 constant_dynamic-update-slice_fusion.14
  157.5 1.9 constant_dynamic-update-slice_fusion.13
  159.4 1.9 constant_dynamic-update-slice_fusion.12
  161.2 1.9 constant_dynamic-update-slice_fusion.11
  163.1 6.5 %collective-permute-done.12 = bf16[512,512]{1,0:T(8,128)(2,1)} collective-permute-done((bf16[512,512]{1,0:T(8,128)(2,1)}, bf16[512,512]{1,0:T(8,128)(2,1)}, u32[]{:S(2)}, u32[]{:S(2)}) %collective-permute-start.12) | collective-permute-done | bytes 524320 | tf_op jit(solution)/shard_map/ppermute | solution.py:36
  169.6 1.9 constant_dynamic-update-slice_fusion.10
  171.5 1.9 constant_dynamic-update-slice_fusion.9
  173.4 1.9 constant_dynamic-update-slice_fusion.8
  175.3 1.9 constant_dynamic-update-slice_fusion.7
  177.2 0.8 constant_dynamic-update-slice_fusion.6
  178.0 3.1 %collective-permute-done.13 = bf16[512,512]{1,0:T(8,128)(2,1)S(1)} collective-permute-done((bf16[512,512]{1,0:T(8,128)(2,1)}, bf16[512,512]{1,0:T(8,128)(2,1)S(1)}, u32[]{:S(2)}, u32[]{:S(2)}) %collective-permute-start.13) | collective-permute-done | bytes 524320 | tf_op jit(solution)/shard_map/ppermute | solution.py:36
  181.1 1.9 constant_dynamic-update-slice_fusion.5
  183.0 1.9 constant_dynamic-update-slice_fusion.4
  184.9 1.9 constant_dynamic-update-slice_fusion.3
  186.7 1.9 constant_dynamic-update-slice_fusion.2
  188.6 0.8 constant_dynamic-update-slice_fusion.1
  189.5 2.9 %collective-permute-done.14 = bf16[512,512]{1,0:T(8,128)(2,1)S(1)} collective-permute-done((bf16[512,512]{1,0:T(8,128)(2,1)S(1)}, bf16[512,512]{1,0:T(8,128)(2,1)S(1)}, u32[]{:S(2)}, u32[]{:S(2)}) %collective-permute-start.14) | collective-permute-done | bytes 524320 | tf_op jit(solution)/shard_map/ppermute | solution.py:36
  192.4 0.8 constant_dynamic-update-slice_fusion
  193.3 6.5 %fusion.27 = bf16[128,512]{0,1:T(8,128)(2,1)} fusion(f32[128,512]{0,1:T(8,128)S(1)} %convolution_multiply_fusion, bf16[8192,512]{1,0:T(8,128)(2,1)} %constant_dynamic-update-slice_fusion, bf16[128,8192]{1,0:T(8,128)(2,1)S(1)} %copy-done), kind=kOutput, calls=%fused_computation.37 | convolution fusion | flops 1073872896 | bytes 10878976 | tf_op jit(solution)/shard_map/dot_general | solution.py:44
  199.8 0.6 dynamic-slice
  201.1 0.2 dynamic-update-slice
  201.3 9.1 %all-reduce = s32[32]{0:T(128)S(1)} all-reduce(s32[32]{0:T(128)S(1)} %dynamic-update-slice), channel_id=1, replica_groups=mesh['group'=2,'ctx'=16] {'ctx'}, use_global_device_ids=true, to_apply=%add | all-reduce | flops 32 | bytes 256
  210.6 0.7 slice_reduce_fusion.1
  211.3 0.7 iota_add_fusion
  214.6 24.6 %all-gather.5.cloned.1.call-done = bf16[2048,512]{0,1:T(8,128)(2,1)} async-done(((bf16[128,512]{0,1:T(8,128)(2,1)}), bf16[2048,512]{0,1:T(8,128)(2,1)}) %all-gather.5.cloned.1.call-update) | async-done | bytes 2097168 | tf_op jit(solution)/shard_map/all_gather | solution.py:77
  239.2 13.6 %conditional.2 = (f32[4,8,64]{2,1,0:T(8,128)S(1)}, f32[4,8,64,128]{3,2,1,0:T(8,128)S(1)}) conditional(s32[]{:T(128)} %convert_element_type.36, () %tuple.21, (s32[1,64]{1,0:T(1,128)S(1)}, s32[32,64]{1,0:T(8,128)S(1)}, bf16[128,4096]{1,0:T(8,128)(2,1)S(1)}, bf16[2048,4,128]{0,2,1:T(8,128)(2,1)}, bf16[2048,4,128]{0,2,1:T(8,128)(2,1)}) %tuple.48), branch_computations={%region_2.3_spmd, %region_3.6_spmd} | conditional | flops 2202138624 | bytes 67182896 | solution.py:106
  239.3 0.1 broadcast_compare_fusion
  239.5 0.1 copy.36
  239.6 4.6 %fusion = (f32[4,8,64]{2,1,0:T(8,128)S(1)}, f32[4,2048,64,8]{1,2,3,0:T(8,128)S(1)}) fusion(pred[64,2048]{1,0:T(8,128)(4,1)S(1)} %broadcast_compare_fusion, bf16[64,4,8,128]{3,2,1,0:T(8,128)(2,1)S(1)} %bitcast.84, bf16[2048,4,128]{0,2,1:T(8,128)(2,1)} %get-tuple-element.62), kind=kOutput, calls=%fused_computation.2 | convolution fusion | flops 1086322688 | bytes 19537920 | tf_op jit(solution)/shard_map/cond/branch_1_fun/tkgd,skd->kgts/dot_general | solution.py:87
  244.2 3.5 %fusion.3 = f32[4,8,64,128]{3,2,1,0:T(8,128)S(1)} fusion(f32[4,2048,64,8]{1,2,3,0:T(8,128)S(1)} %get-tuple-element.72, f32[4,8,64]{2,1,0:T(8,128)S(1)} %broadcast_maximum_fusion, pred[64,2048]{1,0:T(8,128)(4,1)S(1)} %broadcast_compare_fusion, bf16[2048,4,128]{0,2,1:T(8,128)(2,1)S(1)} %copy-done.10), kind=kOutput, calls=%fused_computation.5 | convolution fusion | flops 1094713344 | bytes 20062208 | tf_op jit(solution)/shard_map/cond/branch_1_fun/kgts,skd->kgtd/dot_general | solution.py:95
  247.8 5.1 %fusion.2 = f32[4,8,64]{2,1,0:T(8,128)S(1)} fusion(f32[4,2048,64,8]{1,2,3,0:T(8,128)S(1)} %get-tuple-element.72, f32[4,8,64]{2,1,0:T(8,128)S(1)} %broadcast_maximum_fusion, pred[64,2048]{1,0:T(8,128)(4,1)S(1)} %broadcast_compare_fusion), kind=kLoop, calls=%fused_computation.4 | loop fusion | flops 20969472 | bytes 16924672 | tf_op jit(solution)/shard_map/cond/branch_1_fun/reduce_sum | solution.py:94
  252.8 0.3 fusion.28
  253.2 1.1 copy.19
  254.3 13.6 %conditional.3 = (f32[4,8,64]{2,1,0:T(8,128)S(1)}, f32[4,8,64,128]{3,2,1,0:T(8,128)S(1)}) conditional(s32[]{:T(128)} %convert_element_type.42, () %tuple.23, (s32[1,64]{1,0:T(1,128)S(1)}, s32[32,64]{1,0:T(8,128)S(1)}, bf16[128,4096]{1,0:T(8,128)(2,1)S(1)}, bf16[2048,4,128]{0,2,1:T(8,128)(2,1)}, bf16[2048,4,128]{0,2,1:T(8,128)(2,1)}) %tuple.49), branch_computations={%region_7.8_spmd, %region_8.11_spmd} | conditional | flops 2202138624 | bytes 67182896 | solution.py:106
  254.4 0.1 broadcast_compare_fusion.1
  254.7 4.6 %fusion.13 = (f32[4,8,64]{2,1,0:T(8,128)S(1)}, f32[4,2048,64,8]{1,2,3,0:T(8,128)S(1)}) fusion(pred[64,2048]{1,0:T(8,128)(4,1)S(1)} %broadcast_compare_fusion.1, bf16[64,4,8,128]{3,2,1,0:T(8,128)(2,1)S(1)} %bitcast.85, bf16[2048,4,128]{0,2,1:T(8,128)(2,1)} %get-tuple-element.67), kind=kOutput, calls=%fused_computation.19 | convolution fusion | flops 1086322688 | bytes 19537920 | tf_op jit(solution)/shard_map/cond/branch_1_fun/tkgd,skd->kgts/dot_general | solution.py:87
  259.3 3.5 %fusion.16 = f32[4,8,64,128]{3,2,1,0:T(8,128)S(1)} fusion(f32[4,2048,64,8]{1,2,3,0:T(8,128)S(1)} %get-tuple-element.74, f32[4,8,64]{2,1,0:T(8,128)S(1)} %broadcast_maximum_fusion.1, pred[64,2048]{1,0:T(8,128)(4,1)S(1)} %broadcast_compare_fusion.1, bf16[2048,4,128]{0,2,1:T(8,128)(2,1)S(1)} %copy-done.11), kind=kOutput, calls=%fused_computation.22 | convolution fusion | flops 1094713344 | bytes 20062208 | tf_op jit(solution)/shard_map/cond/branch_1_fun/kgts,skd->kgtd/dot_general | solution.py:95
  262.8 5.1 %fusion.15 = f32[4,8,64]{2,1,0:T(8,128)S(1)} fusion(f32[4,2048,64,8]{1,2,3,0:T(8,128)S(1)} %get-tuple-element.74, f32[4,8,64]{2,1,0:T(8,128)S(1)} %broadcast_maximum_fusion.1, pred[64,2048]{1,0:T(8,128)(4,1)S(1)} %broadcast_compare_fusion.1), kind=kLoop, calls=%fused_computation.21 | loop fusion | flops 20969472 | bytes 16924672 | tf_op jit(solution)/shard_map/cond/branch_1_fun/reduce_sum | solution.py:94
  267.9 0.3 fusion.29
  268.3 0.3 copy.22
  268.6 1.4 copy_bitcast_fusion
  270.0 1.1 pad_maximum_fusion
  (53 shorter events, 0.6 us)
Async XLA Ops:
  6.5 130.3 %copy-start = (bf16[128,8192]{1,0:T(8,128)(2,1)S(1)}, bf16[128,8192]{1,0:T(8,128)(2,1)}, u32[]{:S(2)}) copy-start(bf16[128,8192]{1,0:T(8,128)(2,1)} %param.11) | copy-start | bytes 6291460
  6.5 149.2 %copy-start.3 = (bf16[512,512]{1,0:T(8,128)(2,1)S(1)}, bf16[512,512]{1,0:T(8,128)(2,1)}, u32[]{:S(2)}) copy-start(bf16[512,512]{1,0:T(8,128)(2,1)} %param.14) | copy-start | bytes 1572868
  6.5 208.1 %all-gather.3.cloned.1.call-start = ((), (), s32[]{:S(2)}) async-start(), calls=%async_computation | async-start | bytes 2228224 | tf_op jit(solution)/shard_map/all_gather | solution.py:73
  6.5 12.6 %collective-permute-start = (bf16[512,512]{1,0:T(8,128)(2,1)}, bf16[512,512]{1,0:T(8,128)(2,1)S(1)}, u32[]{:S(2)}, u32[]{:S(2)}) collective-permute-start(bf16[512,512]{1,0:T(8,128)(2,1)} %param.14), channel_id=1, source_target_pairs={{0,1},{1,2},{2,3},{3,4},{4,5},{5,6},{6,7},{7,8},{8,9},{9,10},{10,1... | collective-permute-start | bytes 1572872 | tf_op jit(solution)/shard_map/ppermute | solution.py:36
  19.1 11.4 %collective-permute-start.1 = (bf16[512,512]{1,0:T(8,128)(2,1)S(1)}, bf16[512,512]{1,0:T(8,128)(2,1)}, u32[]{:S(2)}, u32[]{:S(2)}) collective-permute-start(bf16[512,512]{1,0:T(8,128)(2,1)S(1)} %collective-permute-done), channel_id=1, source_target_pairs={{0,1},{1,2},{2,3},{3,4},{4,5},{5,6},{6,7},{7,8},{8,9},{9,10},{10,1... | collective-permute-start | bytes 1572872 | tf_op jit(solution)/shard_map/ppermute | solution.py:36
  30.5 11.6 %collective-permute-start.2 = (bf16[512,512]{1,0:T(8,128)(2,1)}, bf16[512,512]{1,0:T(8,128)(2,1)}, u32[]{:S(2)}, u32[]{:S(2)}) collective-permute-start(bf16[512,512]{1,0:T(8,128)(2,1)} %collective-permute-done.1), channel_id=1, source_target_pairs={{0,1},{1,2},{2,3},{3,4},{4,5},{5,6},{6,7},{7,8},{8,9},{9,10},{10,1... | collective-permute-start | bytes 1572872 | tf_op jit(solution)/shard_map/ppermute | solution.py:36
  42.1 11.5 %collective-permute-start.3 = (bf16[512,512]{1,0:T(8,128)(2,1)}, bf16[512,512]{1,0:T(8,128)(2,1)S(1)}, u32[]{:S(2)}, u32[]{:S(2)}) collective-permute-start(bf16[512,512]{1,0:T(8,128)(2,1)} %collective-permute-done.2), channel_id=1, source_target_pairs={{0,1},{1,2},{2,3},{3,4},{4,5},{5,6},{6,7},{7,8},{8,9},{9,10},{10,1... | collective-permute-start | bytes 1572872 | tf_op jit(solution)/shard_map/ppermute | solution.py:36
  53.7 0.8 copy-start.5
  53.7 11.4 %collective-permute-start.4 = (bf16[512,512]{1,0:T(8,128)(2,1)S(1)}, bf16[512,512]{1,0:T(8,128)(2,1)}, u32[]{:S(2)}, u32[]{:S(2)}) collective-permute-start(bf16[512,512]{1,0:T(8,128)(2,1)S(1)} %collective-permute-done.3), channel_id=1, source_target_pairs={{0,1},{1,2},{2,3},{3,4},{4,5},{5,6},{6,7},{7,8},{8,9},{9,10},{10,1... | collective-permute-start | bytes 1572872 | tf_op jit(solution)/shard_map/ppermute | solution.py:36
  65.1 11.5 %collective-permute-start.5 = (bf16[512,512]{1,0:T(8,128)(2,1)}, bf16[512,512]{1,0:T(8,128)(2,1)S(1)}, u32[]{:S(2)}, u32[]{:S(2)}) collective-permute-start(bf16[512,512]{1,0:T(8,128)(2,1)} %collective-permute-done.4), channel_id=1, source_target_pairs={{0,1},{1,2},{2,3},{3,4},{4,5},{5,6},{6,7},{7,8},{8,9},{9,10},{10,1... | collective-permute-start | bytes 1572872 | tf_op jit(solution)/shard_map/ppermute | solution.py:36
  76.6 0.8 copy-start.4
  77.4 11.3 %collective-permute-start.6 = (bf16[512,512]{1,0:T(8,128)(2,1)S(1)}, bf16[512,512]{1,0:T(8,128)(2,1)S(1)}, u32[]{:S(2)}, u32[]{:S(2)}) collective-permute-start(bf16[512,512]{1,0:T(8,128)(2,1)S(1)} %collective-permute-done.5), channel_id=1, source_target_pairs={{0,1},{1,2},{2,3},{3,4},{4,5},{5,6},{6,7},{7,8},{8,9},{9,10},{10,1... | collective-permute-start | bytes 1572872 | tf_op jit(solution)/shard_map/ppermute | solution.py:36
  88.7 0.8 copy-start.6
  89.5 11.3 %collective-permute-start.7 = (bf16[512,512]{1,0:T(8,128)(2,1)S(1)}, bf16[512,512]{1,0:T(8,128)(2,1)S(1)}, u32[]{:S(2)}, u32[]{:S(2)}) collective-permute-start(bf16[512,512]{1,0:T(8,128)(2,1)S(1)} %collective-permute-done.6), channel_id=1, source_target_pairs={{0,1},{1,2},{2,3},{3,4},{4,5},{5,6},{6,7},{7,8},{8,9},{9,10},{10,1... | collective-permute-start | bytes 1572872 | tf_op jit(solution)/shard_map/ppermute | solution.py:36
  100.8 0.8 copy-start.7
  101.6 11.3 %collective-permute-start.8 = (bf16[512,512]{1,0:T(8,128)(2,1)S(1)}, bf16[512,512]{1,0:T(8,128)(2,1)S(1)}, u32[]{:S(2)}, u32[]{:S(2)}) collective-permute-start(bf16[512,512]{1,0:T(8,128)(2,1)S(1)} %collective-permute-done.7), channel_id=1, source_target_pairs={{0,1},{1,2},{2,3},{3,4},{4,5},{5,6},{6,7},{7,8},{8,9},{9,10},{10,1... | collective-permute-start | bytes 1572872 | tf_op jit(solution)/shard_map/ppermute | solution.py:36
  112.9 0.8 copy-start.8
  113.8 11.4 %collective-permute-start.9 = (bf16[512,512]{1,0:T(8,128)(2,1)S(1)}, bf16[512,512]{1,0:T(8,128)(2,1)}, u32[]{:S(2)}, u32[]{:S(2)}) collective-permute-start(bf16[512,512]{1,0:T(8,128)(2,1)S(1)} %collective-permute-done.8), channel_id=1, source_target_pairs={{0,1},{1,2},{2,3},{3,4},{4,5},{5,6},{6,7},{7,8},{8,9},{9,10},{10,1... | collective-permute-start | bytes 1572872 | tf_op jit(solution)/shard_map/ppermute | solution.py:36
  125.2 11.6 %collective-permute-start.10 = (bf16[512,512]{1,0:T(8,128)(2,1)}, bf16[512,512]{1,0:T(8,128)(2,1)}, u32[]{:S(2)}, u32[]{:S(2)}) collective-permute-start(bf16[512,512]{1,0:T(8,128)(2,1)} %collective-permute-done.9), channel_id=1, source_target_pairs={{0,1},{1,2},{2,3},{3,4},{4,5},{5,6},{6,7},{7,8},{8,9},{9,10},{10,1... | collective-permute-start | bytes 1572872 | tf_op jit(solution)/shard_map/ppermute | solution.py:36
  126.9 112.3 %all-gather.5.cloned.1.call-start = ((), (), s32[]{:S(2)}) async-start(), calls=%async_computation.1 | async-start | bytes 2228224 | tf_op jit(solution)/shard_map/all_gather | solution.py:77
  136.8 15.2 %collective-permute-start.11 = (bf16[512,512]{1,0:T(8,128)(2,1)}, bf16[512,512]{1,0:T(8,128)(2,1)}, u32[]{:S(2)}, u32[]{:S(2)}) collective-permute-start(bf16[512,512]{1,0:T(8,128)(2,1)} %collective-permute-done.10), channel_id=1, source_target_pairs={{0,1},{1,2},{2,3},{3,4},{4,5},{5,6},{6,7},{7,8},{8,9},{9,10},{10,1... | collective-permute-start | bytes 1572872 | tf_op jit(solution)/shard_map/ppermute | solution.py:36
  152.0 17.6 %collective-permute-start.12 = (bf16[512,512]{1,0:T(8,128)(2,1)}, bf16[512,512]{1,0:T(8,128)(2,1)}, u32[]{:S(2)}, u32[]{:S(2)}) collective-permute-start(bf16[512,512]{1,0:T(8,128)(2,1)} %collective-permute-done.11), channel_id=1, source_target_pairs={{0,1},{1,2},{2,3},{3,4},{4,5},{5,6},{6,7},{7,8},{8,9},{9,10},{10,1... | collective-permute-start | bytes 1572872 | tf_op jit(solution)/shard_map/ppermute | solution.py:36
  156.6 20.6 %copy-start.9 = (bf16[512,512]{1,0:T(8,128)(2,1)S(1)}, bf16[512,512]{1,0:T(8,128)(2,1)}, u32[]{:S(2)}) copy-start(bf16[512,512]{1,0:T(8,128)(2,1)} %copy-done.8) | copy-start | bytes 1572868
  169.6 11.5 %collective-permute-start.13 = (bf16[512,512]{1,0:T(8,128)(2,1)}, bf16[512,512]{1,0:T(8,128)(2,1)S(1)}, u32[]{:S(2)}, u32[]{:S(2)}) collective-permute-start(bf16[512,512]{1,0:T(8,128)(2,1)} %collective-permute-done.12), channel_id=1, source_target_pairs={{0,1},{1,2},{2,3},{3,4},{4,5},{5,6},{6,7},{7,8},{8,9},{9,10},{10,1... | collective-permute-start | bytes 1572872 | tf_op jit(solution)/shard_map/ppermute | solution.py:36
  181.1 11.3 %collective-permute-start.14 = (bf16[512,512]{1,0:T(8,128)(2,1)S(1)}, bf16[512,512]{1,0:T(8,128)(2,1)S(1)}, u32[]{:S(2)}, u32[]{:S(2)}) collective-permute-start(bf16[512,512]{1,0:T(8,128)(2,1)S(1)} %collective-permute-done.13), channel_id=1, source_target_pairs={{0,1},{1,2},{2,3},{3,4},{4,5},{5,6},{6,7},{7,8},{8,9},{9,10},{10,1... | collective-permute-start | bytes 1572872 | tf_op jit(solution)/shard_map/ppermute | solution.py:36
  193.3 6.6 %copy-start.13 = (u32[32]{0:T(128)S(1)}, u32[32]{0:T(128)}, u32[]{:S(2)}) copy-start(u32[32]{0:T(128)} %constant.161) | copy-start | bytes 388
  193.3 7.8 %copy-start.12 = (s32[2]{0:T(128)S(1)}, s32[2]{0:T(128)}, u32[]{:S(2)}) copy-start(s32[2]{0:T(128)} %param.17) | copy-start | bytes 28
  193.3 46.0 %copy-start.2 = (bf16[128,4096]{1,0:T(8,128)(2,1)S(1)}, bf16[128,4096]{1,0:T(8,128)(2,1)}, u32[]{:S(2)}) copy-start(bf16[128,4096]{1,0:T(8,128)(2,1)} %param.12) | copy-start | bytes 3145732
  239.6 4.6 %copy-start.10 = (bf16[2048,4,128]{0,2,1:T(8,128)(2,1)S(1)}, bf16[2048,4,128]{0,2,1:T(8,128)(2,1)}, u32[]{:S(2)}) copy-start(bf16[2048,4,128]{0,2,1:T(8,128)(2,1)} %get-tuple-element.63) | copy-start | bytes 6291460 | tf_op jit(solution)/shard_map/cond
  254.7 4.6 %copy-start.11 = (bf16[2048,4,128]{0,2,1:T(8,128)(2,1)S(1)}, bf16[2048,4,128]{0,2,1:T(8,128)(2,1)}, u32[]{:S(2)}) copy-start(bf16[2048,4,128]{0,2,1:T(8,128)(2,1)} %get-tuple-element.68) | copy-start | bytes 6291460 | tf_op jit(solution)/shard_map/cond
  267.9 3.2 %copy-start.1 = (bf16[128,8192]{1,0:T(8,128)(2,1)S(1)}, bf16[128,8192]{1,0:T(8,128)(2,1)}, u32[]{:S(2)}) copy-start(bf16[128,8192]{1,0:T(8,128)(2,1)} %param.11) | copy-start | bytes 6291460
Sparse Core Ops, SparseCore 0:
  127.0 45.7 all-gather.2
  199.9 39.2 all-gather.4
